TPU v7x, 32 devices: a whole 2x2x4 slice. The times are simulated.
32 devices in a mesh: box: 8 (over z, y), nbr: 4 (over x, core).
Axes of the slice: x: 2, y: 2, z: 4, core: 2. Of those that a mesh axis runs over, the one named last changes fastest.
Arguments:
- self_block: float32 [64, 256, 256], P('box', 'nbr'), as said below
- ordering: int32 [64, 256], P('box'), may hold values from 0 to 255, each once within a row
- interp: float32 [64, 64, 192], P('box'), may hold values from -0.12 to 0.12
- near_band: float32 [64, 8, 2, 64, 256], P('box', 'nbr'), may hold values from -3 to 3
- pair_mask: int32 [64, 8], P('box', 'nbr'), may hold values 0 or 1
Outputs:
- skeleton_self: float32 [64, 64, 64], P('box')
- red_inverse: float32 [64, 192, 192], P('box', 'nbr')
- couplings: float32 [64, 8, 64, 128], P('box', 'nbr')
Inputs may be any that keep to these rules, and one draw needn't show every extreme that they name: Each row of ordering is a permutation of the 256 unknowns of its box. Each self_block[b] has a positive diagonal.
All inputs are finite; a program needn't handle non-finite values. No bound on the sum of `pair_mask` on one device may be relied on, other than what follows from the above.
Results may differ from a plain program's by a relative error of at most 0.0003.
Values sent between devices are 32-bit elements; how exact they have to be, the bound alone decides.
A program may use at most 128 MiB of HBM per device.

v0:
```python
import jax
import jax.numpy as jnp
from jax import lax
from jax.sharding import PartitionSpec as P

SKEL = 64
RED = 192
REACH = 4
NS_ITERS = 3


def extended_2(block, sides, width):
    for axis, dim in sides:
        count = lax.axis_size(axis)
        forward = [(i, i + 1) for i in range(count - 1)]
        forward.append((count - 1, 0))
        backward = [(target, source) for source, target in forward]
        low = lax.ppermute(
            lax.slice_in_dim(block, block.shape[dim] - width, None, axis=dim), axis, forward
        )
        high = lax.ppermute(lax.slice_in_dim(block, 0, width, axis=dim), axis, backward)
        block = jnp.concatenate([low, block, high], axis=dim)
    return block


def passed_along(block, axis, distance):
    devices = range(lax.axis_size(axis))
    route = [((i - distance) % len(devices), i) for i in devices]
    return lax.ppermute(block, axis, route)


def product(pattern, left_term, right_term):
    return jnp.einsum(pattern, left_term, right_term, precision=lax.Precision.HIGHEST)


def selector(ordering):
    columns = jnp.arange(ordering.shape[1], dtype=jnp.int32)
    return (ordering[:, :, None] == columns[None, None, :]).astype(jnp.float32)


def permuted(matrix, chooser):
    row_sorted = product("bik,bkj->bij", chooser, matrix)
    return product("bik,bjk->bij", row_sorted, chooser)


def factors(matrix, chooser, interp):
    full_block = permuted(matrix, chooser)
    skel_skel = full_block[:, :SKEL, :SKEL]
    skel_red = full_block[:, :SKEL, SKEL:]
    red_skel = full_block[:, SKEL:, :SKEL]
    red_red = full_block[:, SKEL:, SKEL:]
    skel_interp = product("bij,bjk->bik", skel_skel, interp)
    x_skel_red = skel_red - skel_interp
    x_red_skel = red_skel - product("bji,bjk->bik", interp, skel_skel)
    x_red_red = (
        red_red
        - product("bji,bjk->bik", interp, skel_red)
        - product("bij,bjk->bik", red_skel, interp)
    )
    x_red_red = x_red_red + product("bji,bjk->bik", interp, skel_interp)
    identity = jnp.eye(RED, dtype=jnp.float32)
    diag_vals = jnp.diagonal(red_red, axis1=1, axis2=2)
    approx = identity[None] / diag_vals[:, None, :]
    for sweep_index in range(NS_ITERS):
        approx = 2.0 * approx - product(
            "bij,bjk->bik", approx, product("bij,bjk->bik", x_red_red, approx)
        )
    left_factor = product("bij,bjk->bik", x_skel_red, approx)
    right_factor = product("bij,bjk->bik", approx, x_red_skel)
    own_block = skel_skel - product("bij,bjk->bik", left_factor, x_red_skel)
    return (approx, left_factor, right_factor, own_block)


def slot_terms(near_piece, chooser, interp, approx, left_factor, right_factor):
    both_parts = product("bpik,bjk->bpij", near_piece, chooser)
    row_part = both_parts[:, 0]
    col_part = both_parts[:, 1]
    near_red = row_part[:, :, SKEL:] - product("bij,bjk->bik", row_part[:, :, :SKEL], interp)
    red_near_t = col_part[:, :, SKEL:] - product("bij,bjk->bik", col_part[:, :, :SKEL], interp)
    new_forward = jnp.swapaxes(col_part[:, :, :SKEL], 1, 2) - product(
        "bij,bkj->bik", left_factor, red_near_t
    )
    new_backward = jnp.swapaxes(row_part[:, :, :SKEL], 1, 2) - product(
        "bji,bkj->bik", right_factor, near_red
    )
    coupled = jnp.concatenate([new_forward, new_backward], axis=2)
    update = product("bij,bkj->bik", product("bij,bjk->bik", near_red, approx), red_near_t)
    return (coupled, update)


def body(self_block, ordering, interp, near_band, pair_mask):
    box_count = ordering.shape[0]
    nbr_count = lax.axis_size("nbr")
    nbr_place = lax.axis_index("nbr")
    chooser = selector(ordering)
    share_boxes = box_count // nbr_count
    own_rows = lax.all_to_all(self_block, "nbr", split_axis=0, concat_axis=1, tiled=True)
    my_chooser = lax.dynamic_slice_in_dim(chooser, nbr_place * share_boxes, share_boxes, 0)
    my_interp = lax.dynamic_slice_in_dim(interp, nbr_place * share_boxes, share_boxes, 0)
    part_inverse, part_left, part_right, part_own = factors(own_rows, my_chooser, my_interp)
    approx, left_factor, right_factor, own_block = (
        lax.all_gather(part_inverse, "nbr", axis=0, tiled=True),
        lax.all_gather(part_left, "nbr", axis=0, tiled=True),
        lax.all_gather(part_right, "nbr", axis=0, tiled=True),
        lax.all_gather(part_own, "nbr", axis=0, tiled=True),
    )
    masked = near_band * pair_mask.astype(jnp.float32)[:, :, None, None, None]
    local_slots = near_band.shape[1]
    windows = []
    widened = extended_2(masked, (("box", 0),), REACH)
    for slot_index in range(local_slots):
        windows.append((widened[:, slot_index], REACH))
    extended = jnp.zeros((box_count + 2 * REACH, SKEL, SKEL), jnp.float32)
    couples = []
    for slot_index in range(local_slots):
        window, margin = windows[slot_index]
        global_slot = nbr_place * local_slots + slot_index
        offset = jnp.where(global_slot < REACH, global_slot - REACH, global_slot - REACH + 1)
        near_piece = lax.dynamic_slice_in_dim(window, margin - offset, box_count, 0)
        coupled, update = slot_terms(near_piece, chooser, interp, approx, left_factor, right_factor)
        couples.append(coupled)
        extended = extended + lax.dynamic_update_slice_in_dim(
            jnp.zeros_like(extended), update, REACH - offset, 0
        )
    incoming_right = passed_along(extended[:REACH], "box", -1)
    incoming_left = passed_along(extended[REACH + box_count :], "box", 1)
    owned_sum = extended[REACH : REACH + box_count]
    owned_sum = owned_sum.at[box_count - REACH :].add(incoming_right)
    owned_sum = owned_sum.at[:REACH].add(incoming_left)
    update_total = lax.psum(owned_sum, "nbr")
    skeleton_self = own_block - update_total
    row_count = approx.shape[1] // nbr_count
    red_inverse = lax.dynamic_slice_in_dim(approx, nbr_place * row_count, row_count, 1)
    return (skeleton_self, red_inverse, jnp.stack(couples, 1))


def solution(mesh):
    placed = (
        P("box", "nbr", None),
        P("box", None),
        P("box", None, None),
        P("box", "nbr", None, None, None),
        P("box", "nbr"),
    )
    return jax.shard_map(
        body,
        mesh=mesh,
        in_specs=placed,
        out_specs=(P("box", None, None), P("box", "nbr", None), P("box", "nbr", None, None)),
        check_vma=False,
    )
```

profile of v0, /device:TPU:0, one launch (start us, length us, event | category | flops | bytes accessed | tf_op | source)
XLA Modules:
  0.0 154.4 jit_solution(4811347467437603980)
XLA Ops:
  7.2 4.4 %all-to-all-start = ((f32[8,64,256]{2,1,0:T(8,128)}), f32[8,64,256]{2,1,0:T(8,128)S(1)}, u32[]{:S(2)}, u32[]{:S(2)}) async-start(f32[8,64,256]{2,1,0:T(8,128)} %param.9), calls=%async_computation | async-start | bytes 1048576 | tf_op jit(solution)/shard_map/all_to_all | solution.py:97
  11.6 0.7 convert_element_type.12
  12.2 0.1 copy.79
  12.3 1.9 %broadcast_multiply_fusion = f32[8,2,2,64,256]{4,3,2,1,0:T(8,128)S(1)} fusion(f32[8,2,2,64,256]{4,3,2,1,0:T(8,128)} %param.12, f32[8,2]{1,0:T(8,128)S(1)} %copy.79), kind=kLoop, calls=%fused_computation.31 | loop fusion | flops 524288 | bytes 4194368 | tf_op jit(solution)/shard_map/mul | solution.py:107
  14.2 1.5 fusion.50
  15.8 2.3 %collective-permute-start = (f32[4,2,2,64,256]{4,3,2,1,0:T(8,128)}, f32[4,2,2,64,256]{4,3,2,1,0:T(8,128)}, u32[]{:S(2)}, u32[]{:S(2)}) collective-permute-start(f32[4,2,2,64,256]{4,3,2,1,0:T(8,128)} %get-tuple-element.44), channel_id=1, source_target_pairs={{0,4},{4,8},{8,12},{12,16},{16,20},{20,24},{24,28},{28,0},{1,5},{5... | collective-permute-start | bytes 3145736 | tf_op jit(solution)/shard_map/ppermute | solution.py:18
  18.1 3.0 %collective-permute-start.1 = (f32[4,2,2,64,256]{4,3,2,1,0:T(8,128)}, f32[4,2,2,64,256]{4,3,2,1,0:T(8,128)}, u32[]{:S(2)}, u32[]{:S(2)}) collective-permute-start(f32[4,2,2,64,256]{4,3,2,1,0:T(8,128)} %get-tuple-element.45), channel_id=1, source_target_pairs={{4,0},{8,4},{12,8},{16,12},{20,16},{24,20},{28,24},{0,28},{5,1},{9... | collective-permute-start | bytes 3145736 | tf_op jit(solution)/shard_map/ppermute | solution.py:21
  21.1 0.7 fusion.25
  21.8 1.1 iota_compare_fusion
  23.0 1.4 fusion.12
  24.3 1.3 fusion.10
  25.7 0.6 convolution_subtract_fusion.5
  26.3 0.9 fusion.36
  27.2 0.9 slice.151
  28.1 0.7 slice.152
  28.8 0.5 convolution_subtract_fusion.4
  29.3 10.5 %copy.75 = f32[2,192,192]{0,2,1:T(8,128)} copy(f32[2,192,192]{2,1,0:T(8,128)} %slice.151) | data formatting | bytes 589824 | tf_op jit(solution)/shard_map/slice | solution.py:51
  39.8 5.2 %gather_fusion = f32[192,2]{1,0:T(8,128)} fusion(f32[2,192,192]{0,2,1:T(8,128)} %copy.75, s32[192]{0:T(256)S(1)} %bitcast.80), kind=kCustom, calls=%fused_computation | custom fusion | bytes 4608 | tf_op jit(solution)/shard_map/jit(diagonal)/gather | solution.py:62
  45.0 1.0 copy.76
  46.0 1.5 convolution_add_fusion
  47.5 1.5 fusion.14
  49.0 0.6 convolution_subtract_fusion.8
  49.5 0.5 fusion.52
  50.1 0.5 convolution_subtract_fusion.7
  50.6 0.5 fusion.53
  51.2 0.5 convolution_subtract_fusion.6
  51.7 2.1 %fusion.28 = f32[2,64,192]{2,1,0:T(8,128)} fusion(f32[2,192,192]{2,1,0:T(8,128)S(1)} %convolution_subtract_fusion.6, f32[2,64,192]{2,1,0:T(8,128)} %fusion.36, f32[2,256,256]{2,1,0:T(8,128)S(1)} %fusion.10), kind=kOutput, calls=%fused_computation.61 | convolution fusion | flops 56647680 | bytes 720896 | tf_op jit(solution)/shard_map/bij,bjk->bik/dot_general | solution.py:33
  53.8 0.0 all-reduce.2.cloned.1.call-start
  53.9 1.8 %copy.96 = f32[2,192,64]{1,2,0:T(8,128)} copy(f32[2,192,64]{2,1,0:T(8,128)} %slice.152) | data formatting | bytes 196608
  55.6 1.2 convolution_subtract_fusion.13
  56.9 1.2 convolution_subtract_fusion.14
  58.0 7.4 %all_gather.12 = f32[8,64,64]{2,1,0:T(8,128)} all-gather(f32[2,64,64]{2,1,0:T(8,128)S(1)} %convolution_subtract_fusion.14), channel_id=1, replica_groups=mesh['box'=8,'nbr'=4] {'nbr'}, dimensions={0}, use_global_device_ids=true | all-gather | bytes 163840 | tf_op jit(solution)/shard_map/all_gather | solution.py:105
  65.4 10.1 %all_gather.14 = f32[8,64,192]{2,1,0:T(8,128)S(1)} all-gather(f32[2,64,192]{2,1,0:T(8,128)} %fusion.28), channel_id=1, replica_groups=mesh['box'=8,'nbr'=4] {'nbr'}, dimensions={0}, use_global_device_ids=true | all-gather | bytes 491520 | tf_op jit(solution)/shard_map/all_gather | solution.py:103
  75.5 0.5 fusion.56
  76.0 7.5 %all_gather.15 = f32[8,192,64]{1,2,0:T(8,128)S(1)} all-gather(f32[2,192,64]{1,2,0:T(8,128)S(1)} %fusion.56), channel_id=1, replica_groups=mesh['box'=8,'nbr'=4] {'nbr'}, dimensions={0}, use_global_device_ids=true | all-gather | bytes 491520 | tf_op jit(solution)/shard_map/all_gather | solution.py:104
  83.5 2.0 %pad_maximum_fusion = f32[16,2,2,64,256]{4,3,2,1,0:T(8,128)S(1)} fusion(f32[4,2,2,64,256]{4,3,2,1,0:T(8,128)} %collective-permute-done.1, f32[8,2,2,64,256]{4,3,2,1,0:T(8,128)S(1)} %broadcast_multiply_fusion, f32[4,2,2,64,256]{4,3,2,1,0:T(8,128)} %collective-permute-done), kind=kLoop, calls=%fused_computation.1 | loop fusion | flops 2097152 | bytes 8388608 | tf_op jit(solution)/shard_map/concatenate | solution.py:22
  85.5 0.4 fusion.49
  85.9 1.6 %fusion.2 = f32[8,2,64,256]{3,2,0,1:T(8,128)S(1)} fusion(s32[8,256]{1,0:T(8,128)S(1)} %copy-done.14, f32[16,1,2,64,256]{4,3,2,1,0:T(8,128)S(1)} %get-tuple-element.42, s32[]{:T(128)S(6)} %select_n.30), kind=kOutput, calls=%fused_computation.5 | convolution fusion | flops 805830656 | bytes 2105348 | tf_op jit(solution)/shard_map/bpik,bjk->bpij/dot_general | solution.py:33
  87.5 0.1 slice_bitcast_fusion
  87.6 0.6 convolution_subtract_fusion
  88.2 1.6 %fusion = f32[8,2,64,256]{3,2,1,0:T(8,128)S(1)} fusion(f32[16,1,2,64,256]{4,3,2,1,0:T(8,128)S(1)} %get-tuple-element.43, s32[]{:T(128)S(6)} %select_n.28, s32[8,256]{1,0:T(8,128)S(1)} %copy-done.14), kind=kOutput, calls=%fused_computation.3 | convolution fusion | flops 805830656 | bytes 2105348 | tf_op jit(solution)/shard_map/bpik,bjk->bpij/dot_general | solution.py:33
  89.8 0.1 slice_bitcast_fusion.2
  89.9 0.6 convolution_subtract_fusion.1
  90.5 0.6 convolution_subtract_fusion.2
  91.1 0.6 convolution_subtract_fusion.3
  91.7 0.7 convolution_subtract_fusion.10
  92.4 0.7 convolution_subtract_fusion.12
  93.0 0.7 convolution_subtract_fusion.9
  93.7 0.7 convolution_subtract_fusion.11
  94.4 1.1 maximum_bitcast_fusion
  95.5 2.8 %fusion.54 = f32[8,64,192]{2,1,0:T(8,128)S(1)} fusion(f32[8,64,192]{2,1,0:T(8,128)} %copy-done.4, f32[8,192,192]{2,1,0:T(8,128)} %all-gather.2.cloned.1.call-done), kind=kOutput, calls=%fused_computation.89 | convolution fusion | flops 226492416 | bytes 1966080 | tf_op jit(solution)/shard_map/bij,bjk->bik/dot_general | solution.py:33
  98.3 0.6 convolution_dynamic-update-slice_fusion
  99.0 1.1 fusion.55
  100.2 0.6 fusion.4
  100.8 0.8 copy-done.7
  101.7 2.3 %collective-permute-start.2 = (f32[4,64,64]{2,1,0:T(8,128)S(1)}, f32[4,64,64]{2,1,0:T(8,128)S(1)}, u32[]{:S(2)}, u32[]{:S(2)}) collective-permute-start(f32[4,64,64]{2,1,0:T(8,128)S(1)} %get-tuple-element.51), channel_id=1, source_target_pairs={{4,0},{8,4},{12,8},{16,12},{20,16},{24,20},{28,24},{0,28},{5,1},{9... | collective-permute-start | bytes 196616 | tf_op jit(solution)/shard_map/ppermute | solution.py:29
  103.9 1.1 pad_maximum_fusion.1
  105.0 2.4 %copy.87 = f32[8,2,64,128]{3,2,1,0:T(8,128)} copy(f32[8,2,64,128]{2,3,0,1:T(8,128)} %pad_maximum_fusion.1) | data formatting | bytes 1048576
  107.4 0.1 collective-permute-start.3
  107.5 8.1 %collective-permute-done.3 = f32[4,64,64]{2,1,0:T(8,128)S(1)} collective-permute-done((f32[4,64,64]{2,1,0:T(8,128)S(1)}, f32[4,64,64]{2,1,0:T(8,128)S(1)}, u32[]{:S(2)}, u32[]{:S(2)}) %collective-permute-start.3) | collective-permute-done | bytes 65568 | tf_op jit(solution)/shard_map/ppermute | solution.py:29
  115.7 0.7 copy-done.11
  116.4 0.8 constant_dynamic-slice_fusion
  117.2 28.7 %all-reduce.2.cloned.1.call-done = f32[8,64,64]{2,1,0:T(8,128)} async-done(((f32[8,64,64]{2,1,0:T(8,128)}), f32[8,64,64]{2,1,0:T(8,128)}) %all-reduce.2.cloned.1.call-update) | async-done | bytes 131088 | tf_op jit(solution)/shard_map/psum | solution.py:130
  145.9 1.7 %sub.80 = f32[8,64,64]{2,1,0:T(8,128)} subtract(f32[8,64,64]{2,1,0:T(8,128)S(1)} %copy-done.12, f32[8,64,64]{2,1,0:T(8,128)} %all-reduce.2.cloned.1.call-done) | non-fusion elementwise | flops 32768 | bytes 393216 | tf_op jit(solution)/shard_map/sub | solution.py:131
  (43 shorter events, 0.3 us)
Async XLA Ops:
  7.2 18.5 %copy-start = (f32[8,64,192]{2,1,0:T(8,128)S(1)}, f32[8,64,192]{2,1,0:T(8,128)}, u32[]{:S(2)}) copy-start(f32[8,64,192]{2,1,0:T(8,128)} %param.11) | copy-start | bytes 1179652
  7.2 15.8 %all-to-all-start = ((f32[8,64,256]{2,1,0:T(8,128)}), f32[8,64,256]{2,1,0:T(8,128)S(1)}, u32[]{:S(2)}, u32[]{:S(2)}) async-start(f32[8,64,256]{2,1,0:T(8,128)} %param.9), calls=%async_computation | async-start | bytes 1048576 | tf_op jit(solution)/shard_map/all_to_all | solution.py:97
  11.6 83.9 %all-gather.2.cloned.1.call-start = ((), (), s32[]{:S(2)}) async-start(), calls=%async_computation.1 | async-start | bytes 1966080 | tf_op jit(solution)/shard_map/all_gather | solution.py:102
  14.2 7.6 %copy-start.14 = (s32[8,256]{1,0:T(8,128)S(1)}, s32[8,256]{1,0:T(8,128)}, u32[]{:S(2)}) copy-start(s32[8,256]{1,0:T(8,128)} %param.10) | copy-start | bytes 24580
  15.8 67.7 %collective-permute-start = (f32[4,2,2,64,256]{4,3,2,1,0:T(8,128)}, f32[4,2,2,64,256]{4,3,2,1,0:T(8,128)}, u32[]{:S(2)}, u32[]{:S(2)}) collective-permute-start(f32[4,2,2,64,256]{4,3,2,1,0:T(8,128)} %get-tuple-element.44), channel_id=1, source_target_pairs={{0,4},{4,8},{8,12},{12,16},{16,20},{20,24},{24,28},{28,0},{1,5},{5... | collective-permute-start | bytes 3145736 | tf_op jit(solution)/shard_map/ppermute | solution.py:18
  18.1 65.4 %collective-permute-start.1 = (f32[4,2,2,64,256]{4,3,2,1,0:T(8,128)}, f32[4,2,2,64,256]{4,3,2,1,0:T(8,128)}, u32[]{:S(2)}, u32[]{:S(2)}) collective-permute-start(f32[4,2,2,64,256]{4,3,2,1,0:T(8,128)} %get-tuple-element.45), channel_id=1, source_target_pairs={{4,0},{8,4},{12,8},{16,12},{20,16},{24,20},{28,24},{0,28},{5,1},{9... | collective-permute-start | bytes 3145736 | tf_op jit(solution)/shard_map/ppermute | solution.py:21
  46.0 3.0 %copy-start.13 = (f32[192,192]{1,0:T(8,128)S(1)}, f32[192,192]{1,0:T(8,128)}, u32[]{:S(2)}) copy-start(f32[192,192]{1,0:T(8,128)} %fusion.25) | copy-start | bytes 442372
  51.7 2.1 %copy-start.2 = (f32[2,192,192]{2,1,0:T(8,128)}, f32[2,192,192]{2,1,0:T(8,128)S(1)}, u32[]{:S(2)}) copy-start(f32[2,192,192]{2,1,0:T(8,128)S(1)} %convolution_subtract_fusion.6) | copy-start | bytes 884740
  53.8 21.7 %copy-start.3 = (f32[2,192,192]{2,1,0:T(8,128)S(1)}, f32[2,192,192]{2,1,0:T(8,128)}, u32[]{:S(2)}) copy-start(f32[2,192,192]{2,1,0:T(8,128)} %copy-done.2) | copy-start | bytes 884740
  53.8 92.0 %all-reduce.2.cloned.1.call-start = ((), (), s32[]{:S(2)}) async-start(), calls=%async_computation.2 | async-start | bytes 524288 | tf_op jit(solution)/shard_map/psum | solution.py:130
  88.2 3.5 %copy-start.5 = (f32[8,64,192]{2,1,0:T(8,128)}, f32[8,64,192]{2,1,0:T(8,128)S(1)}, u32[]{:S(2)}) copy-start(f32[8,64,192]{2,1,0:T(8,128)S(1)} %convolution_subtract_fusion) | copy-start | bytes 1179652
  91.7 2.0 %copy-start.4 = (f32[8,64,192]{2,1,0:T(8,128)}, f32[8,64,192]{2,1,0:T(8,128)S(1)}, u32[]{:S(2)}) copy-start(f32[8,64,192]{2,1,0:T(8,128)S(1)} %convolution_subtract_fusion.3) | copy-start | bytes 1179652
  95.5 3.5 %copy-start.1 = (f32[8,192,192]{2,1,0:T(8,128)S(1)}, f32[8,192,192]{2,1,0:T(8,128)}, u32[]{:S(2)}) copy-start(f32[8,192,192]{2,1,0:T(8,128)} %all-gather.2.cloned.1.call-done) | copy-start | bytes 3538948
  98.3 1.8 %copy-start.6 = (f32[8,64,192]{2,1,0:T(8,128)S(1)}, f32[8,64,192]{2,1,0:T(8,128)}, u32[]{:S(2)}) copy-start(f32[8,64,192]{2,1,0:T(8,128)} %copy-done.5) | copy-start | bytes 1179652
  99.0 4.9 %copy-start.9 = (f32[8,1,64,128]{2,3,0,1:T(8,128)S(1)}, f32[8,1,64,128]{2,3,0,1:T(8,128)}, u32[]{:S(2)}) copy-start(f32[8,1,64,128]{2,3,0,1:T(8,128)} %get-tuple-element.52) | copy-start | bytes 786436
  99.0 4.9 %copy-start.10 = (f32[8,1,64,128]{2,3,0,1:T(8,128)S(1)}, f32[8,1,64,128]{2,3,0,1:T(8,128)}, u32[]{:S(2)}) copy-start(f32[8,1,64,128]{2,3,0,1:T(8,128)} %get-tuple-element.53) | copy-start | bytes 786436
  100.8 0.8 copy-start.7
  101.7 5.7 %copy-start.8 = (f32[16,64,64]{2,1,0:T(8,128)S(1)}, f32[16,64,64]{2,1,0:T(8,128)}, u32[]{:S(2)}) copy-start(f32[16,64,64]{2,1,0:T(8,128)} %copy-done.7) | copy-start | bytes 786436
  101.7 5.8 %collective-permute-start.2 = (f32[4,64,64]{2,1,0:T(8,128)S(1)}, f32[4,64,64]{2,1,0:T(8,128)S(1)}, u32[]{:S(2)}, u32[]{:S(2)}) collective-permute-start(f32[4,64,64]{2,1,0:T(8,128)S(1)} %get-tuple-element.51), channel_id=1, source_target_pairs={{4,0},{8,4},{12,8},{16,12},{20,16},{24,20},{28,24},{0,28},{5,1},{9... | collective-permute-start | bytes 196616 | tf_op jit(solution)/shard_map/ppermute | solution.py:29
  105.0 40.9 %copy-start.12 = (f32[8,64,64]{2,1,0:T(8,128)S(1)}, f32[8,64,64]{2,1,0:T(8,128)}, u32[]{:S(2)}) copy-start(f32[8,64,64]{2,1,0:T(8,128)} %all_gather.12) | copy-start | bytes 393220
  107.4 8.2 %collective-permute-start.3 = (f32[4,64,64]{2,1,0:T(8,128)S(1)}, f32[4,64,64]{2,1,0:T(8,128)S(1)}, u32[]{:S(2)}, u32[]{:S(2)}) collective-permute-start(f32[4,64,64]{2,1,0:T(8,128)S(1)} %get-tuple-element.50), channel_id=1, source_target_pairs={{28,0},{0,4},{4,8},{8,12},{12,16},{16,20},{20,24},{24,28},{29,1},{... | collective-permute-start | bytes 196616 | tf_op jit(solution)/shard_map/ppermute | solution.py:29
  115.7 0.7 copy-start.11
Sparse Core Ops, SparseCore 0:
  53.9 20.9 all-gather.1
  116.5 29.3 all-reduce.1
where the time goes:
time: 155 us; the launch traced here: 154 us
  waiting for transfers between devices  36.9 us (24%)
  matrix products  28.6 us (18%)
  local copies, waits for them, and re-layouts  27.1 us (17%)
  blocking collectives  24.9 us (16%)
  between operations  14.5 us (9%)
  starting transfers between devices  12.1 us (8%)
  other arithmetic  10.3 us (7%)
    psum x1, waiting for transfers between devices, body(): update_total = lax.psum(owned_sum, 'nbr')  28.7 us
    dot_general x30, matrix products, product(): jnp.einsum(pattern, left_term, right_term, precision=lax.Precision.HIGHEST)  28.6 us
    slice x2, local copies, waits for them, and re-layouts, factors(): red_red = full_block[:, SKEL:, SKEL:]  11.4 us
    all_gather x1, blocking collectives, body(): lax.all_gather(part_left, 'nbr', axis=0, tiled=True)  10.1 us
    ppermute x2, waiting for transfers between devices, passed_along(): return lax.ppermute(block, axis, route)  8.12 us
    all_gather x1, blocking collectives, body(): lax.all_gather(part_right, 'nbr', axis=0, tiled=True)  7.46 us
    all_gather x1, blocking collectives, body(): lax.all_gather(part_own, 'nbr', axis=0, tiled=True)  7.4 us
    unnamed x33, local copies, waits for them, and re-layouts  6.4 us
  transfers between devices with their start and end apart: 7, of which 2 were waited for; matrix products, arithmetic and copies ran while one was open for 37% of the time, Pallas kernels for 0%

commit v1 on v0

--- a/solution.py
+++ b/solution.py
@@ -127,7 +127,13 @@
     owned_sum = extended[REACH : REACH + box_count]
     owned_sum = owned_sum.at[box_count - REACH :].add(incoming_right)
     owned_sum = owned_sum.at[:REACH].add(incoming_left)
-    update_total = lax.psum(owned_sum, "nbr")
+    n_dev = lax.axis_size("nbr")
+    update_total, far = (owned_sum, 1)
+    while far < n_dev:
+        update_total = update_total + lax.ppermute(
+            update_total, "nbr", [(i_2, i_2 ^ far) for i_2 in range(n_dev)]
+        )
+        far = 2 * far
     skeleton_self = own_block - update_total
     row_count = approx.shape[1] // nbr_count
     red_inverse = lax.dynamic_slice_in_dim(approx, nbr_place * row_count, row_count, 1)

time: 155 us -> 130 us (0.84)
  waiting for transfers between devices: 36.9 us -> 12.4 us
  other arithmetic: 10.3 us -> 8.41 us
    psum x1 -> x0, waiting for transfers between devices: 28.7 us -> none  [body(): update_total = lax.psum(owned_sum, 'nbr')]
    ppermute x0 -> x2, waiting for transfers between devices: none -> 4.26 us  [body(): lax.ppermute(update_total, 'nbr', [(i_2, i_2 ^ far) for i_2 in range(n_de...]
    unnamed x33 -> x37, local copies, waits for them, and re-layouts: 6.4 us -> 4.87 us
  transfers between devices with their start and end apart: 7 -> 8, of which waited for: 2 -> 4; matrix products, arithmetic and copies ran while one was open for 37% -> 45% of each run, Pallas kernels for 0% -> 0%
where the time goes in v1:
time: 130 us; the launch traced here: 129 us
  matrix products  29.9 us (23%)
  local copies, waits for them, and re-layouts  25.6 us (20%)
  blocking collectives  24.9 us (19%)
  between operations  14.5 us (11%)
  starting transfers between devices  13.4 us (10%)
  waiting for transfers between devices  12.4 us (10%)
  other arithmetic  8.41 us (6%)
    dot_general x30, matrix products, product(): jnp.einsum(pattern, left_term, right_term, precision=lax.Precision.HIGHEST)  29.9 us
    slice x2, local copies, waits for them, and re-layouts, factors(): red_red = full_block[:, SKEL:, SKEL:]  11.4 us
    all_gather x1, blocking collectives, body(): lax.all_gather(part_left, 'nbr', axis=0, tiled=True)  10.1 us
    ppermute x2, waiting for transfers between devices, passed_along(): return lax.ppermute(block, axis, route)  8.13 us
    all_gather x1, blocking collectives, body(): lax.all_gather(part_right, 'nbr', axis=0, tiled=True)  7.46 us
    all_gather x1, blocking collectives, body(): lax.all_gather(part_own, 'nbr', axis=0, tiled=True)  7.37 us
    gather x2, local copies, waits for them, and re-layouts, factors(): diag_vals = jnp.diagonal(red_red, axis1=1, axis2=2)  6.28 us
    unnamed x37, local copies, waits for them, and re-layouts  4.87 us
  transfers between devices with their start and end apart: 8, of which 4 were waited for; matrix products, arithmetic and copies ran while one was open for 45% of the time, Pallas kernels for 0%

profile of v1, /device:TPU:0, one launch (start us, length us, event | category | flops | bytes accessed | tf_op | source)
XLA Modules:
  0.0 129.2 jit_solution(12754254190852601218)
XLA Ops:
  7.2 4.4 %all-to-all-start = ((f32[8,64,256]{2,1,0:T(8,128)}), f32[8,64,256]{2,1,0:T(8,128)S(1)}, u32[]{:S(2)}, u32[]{:S(2)}) async-start(f32[8,64,256]{2,1,0:T(8,128)} %param.9), calls=%async_computation | async-start | bytes 1048576 | tf_op jit(solution)/shard_map/all_to_all | solution.py:97
  11.6 0.7 convert_element_type.12
  12.2 0.1 copy.79
  12.3 1.9 %broadcast_multiply_fusion = f32[8,2,2,64,256]{4,3,2,1,0:T(8,128)S(1)} fusion(f32[8,2,2,64,256]{4,3,2,1,0:T(8,128)} %param.12, f32[8,2]{1,0:T(8,128)S(1)} %copy.79), kind=kLoop, calls=%fused_computation.31 | loop fusion | flops 524288 | bytes 4194368 | tf_op jit(solution)/shard_map/mul | solution.py:107
  14.2 1.5 %fusion.50 = (f32[4,2,2,64,256]{4,3,2,1,0:T(8,128)}, f32[4,2,2,64,256]{4,3,2,1,0:T(8,128)}) fusion(f32[8,2,2,64,256]{4,3,2,1,0:T(8,128)S(1)} %broadcast_multiply_fusion), kind=kLoop, calls=%fused_computation.86 | loop fusion | bytes 4194304 | tf_op jit(solution)/shard_map/slice | solution.py:19
  15.8 2.3 %collective-permute-start = (f32[4,2,2,64,256]{4,3,2,1,0:T(8,128)}, f32[4,2,2,64,256]{4,3,2,1,0:T(8,128)}, u32[]{:S(2)}, u32[]{:S(2)}) collective-permute-start(f32[4,2,2,64,256]{4,3,2,1,0:T(8,128)} %get-tuple-element.44), channel_id=1, source_target_pairs={{0,4},{4,8},{8,12},{12,16},{16,20},{20,24},{24,28},{28,0},{1,5},{5... | collective-permute-start | bytes 3145736 | tf_op jit(solution)/shard_map/ppermute | solution.py:18
  18.1 3.0 %collective-permute-start.1 = (f32[4,2,2,64,256]{4,3,2,1,0:T(8,128)}, f32[4,2,2,64,256]{4,3,2,1,0:T(8,128)}, u32[]{:S(2)}, u32[]{:S(2)}) collective-permute-start(f32[4,2,2,64,256]{4,3,2,1,0:T(8,128)} %get-tuple-element.45), channel_id=1, source_target_pairs={{4,0},{8,4},{12,8},{16,12},{20,16},{24,20},{28,24},{0,28},{5,1},{9... | collective-permute-start | bytes 3145736 | tf_op jit(solution)/shard_map/ppermute | solution.py:21
  21.1 0.7 fusion.25
  21.8 1.1 iota_compare_fusion
  23.0 1.4 %fusion.12 = f32[2,256,256]{2,1,0:T(8,128)S(1)} fusion(f32[2,256,256]{2,1,0:T(8,128)S(1)} %bitcast.82, pred[8,256,256]{2,1,0:T(32,128)(4,1)} %iota_compare_fusion, s32[]{:T(128)S(6)} %select_n.26), kind=kOutput, calls=%fused_computation.42 | convolution fusion | flops 402653184 | bytes 1179652 | tf_op jit(solution)/shard_map/bik,bkj->bij/dot_general | solution.py:33
  24.4 1.3 %fusion.10 = f32[2,256,256]{2,1,0:T(8,128)S(1)} fusion(f32[2,256,256]{2,1,0:T(8,128)S(1)} %fusion.12, pred[8,256,256]{2,1,0:T(32,128)(4,1)} %iota_compare_fusion, s32[]{:T(128)S(6)} %select_n.26), kind=kOutput, calls=%fused_computation.40 | convolution fusion | flops 402653184 | bytes 1179652 | tf_op jit(solution)/shard_map/bik,bjk->bij/dot_general | solution.py:33
  25.7 0.6 convolution_subtract_fusion.5
  26.3 0.9 fusion.36
  27.2 0.9 slice.151
  28.1 0.7 slice.152
  28.8 0.5 convolution_subtract_fusion.4
  29.3 10.5 %copy.75 = f32[2,192,192]{0,2,1:T(8,128)} copy(f32[2,192,192]{2,1,0:T(8,128)} %slice.151) | data formatting | bytes 589824 | tf_op jit(solution)/shard_map/slice | solution.py:51
  39.8 5.3 %gather_fusion = f32[192,2]{1,0:T(8,128)} fusion(f32[2,192,192]{0,2,1:T(8,128)} %copy.75, s32[192]{0:T(256)S(1)} %bitcast.80), kind=kCustom, calls=%fused_computation | custom fusion | bytes 4608 | tf_op jit(solution)/shard_map/jit(diagonal)/gather | solution.py:62
  45.1 1.0 copy.76
  46.0 1.5 %convolution_add_fusion = f32[2,192,192]{2,1,0:T(8,128)S(1)} fusion(f32[2,192,192]{2,1,0:T(8,128)S(1)} %convolution_subtract_fusion.4, f32[2,64,192]{2,1,0:T(8,128)} %fusion.36, f32[8,64,192]{2,1,0:T(8,128)S(1)} %copy-done, s32[]{:T(128)S(6)} %select_n.26), kind=kOutput, calls=%fused_computation.12 | convolution fusion | flops 56696832 | bytes 917508 | tf_op jit(solution)/shard_map/bji,bjk->bik/dot_general | solution.py:33
  47.5 1.5 %fusion.14 = f32[2,192,192]{2,1,0:T(8,128)S(1)} fusion(f32[2,192,192]{2,1,0:T(8,128)S(1)} %convolution_add_fusion, f32[2,192]{1,0:T(2,128)S(1)} %copy.76, f32[192,192]{1,0:T(8,128)} %fusion.25), kind=kOutput, calls=%fused_computation.44 | convolution fusion | flops 169943040 | bytes 738816 | tf_op jit(solution)/shard_map/bij,bjk->bik/dot_general | solution.py:33
  49.0 0.6 convolution_subtract_fusion.8
  49.6 0.5 fusion.52
  50.1 0.5 convolution_subtract_fusion.7
  50.7 0.5 fusion.53
  51.2 0.5 convolution_subtract_fusion.6
  51.8 2.1 %fusion.28 = f32[2,64,192]{2,1,0:T(8,128)} fusion(f32[2,192,192]{2,1,0:T(8,128)S(1)} %convolution_subtract_fusion.6, f32[2,64,192]{2,1,0:T(8,128)} %fusion.36, f32[2,256,256]{2,1,0:T(8,128)S(1)} %fusion.10), kind=kOutput, calls=%fused_computation.62 | convolution fusion | flops 56647680 | bytes 720896 | tf_op jit(solution)/shard_map/bij,bjk->bik/dot_general | solution.py:33
  53.9 1.8 %copy.96 = f32[2,192,64]{1,2,0:T(8,128)} copy(f32[2,192,64]{2,1,0:T(8,128)} %slice.152) | data formatting | bytes 196608
  55.7 1.2 convolution_subtract_fusion.13
  56.9 1.2 convolution_subtract_fusion.14
  58.1 7.4 %all_gather.12 = f32[8,64,64]{2,1,0:T(8,128)} all-gather(f32[2,64,64]{2,1,0:T(8,128)S(1)} %convolution_subtract_fusion.14), channel_id=1, replica_groups=mesh['box'=8,'nbr'=4] {'nbr'}, dimensions={0}, use_global_device_ids=true | all-gather | bytes 163840 | tf_op jit(solution)/shard_map/all_gather | solution.py:105
  65.4 10.1 %all_gather.14 = f32[8,64,192]{2,1,0:T(8,128)S(1)} all-gather(f32[2,64,192]{2,1,0:T(8,128)} %fusion.28), channel_id=1, replica_groups=mesh['box'=8,'nbr'=4] {'nbr'}, dimensions={0}, use_global_device_ids=true | all-gather | bytes 491520 | tf_op jit(solution)/shard_map/all_gather | solution.py:103
  75.5 0.5 fusion.56
  76.1 7.5 %all_gather.15 = f32[8,192,64]{1,2,0:T(8,128)S(1)} all-gather(f32[2,192,64]{1,2,0:T(8,128)S(1)} %fusion.56), channel_id=1, replica_groups=mesh['box'=8,'nbr'=4] {'nbr'}, dimensions={0}, use_global_device_ids=true | all-gather | bytes 491520 | tf_op jit(solution)/shard_map/all_gather | solution.py:104
  83.5 2.0 %pad_maximum_fusion = f32[16,2,2,64,256]{4,3,2,1,0:T(8,128)S(1)} fusion(f32[4,2,2,64,256]{4,3,2,1,0:T(8,128)} %collective-permute-done.1, f32[8,2,2,64,256]{4,3,2,1,0:T(8,128)S(1)} %broadcast_multiply_fusion, f32[4,2,2,64,256]{4,3,2,1,0:T(8,128)} %collective-permute-done), kind=kLoop, calls=%fused_computation.1 | loop fusion | flops 2097152 | bytes 8388608 | tf_op jit(solution)/shard_map/concatenate | solution.py:22
  85.6 0.4 fusion.49
  86.0 1.6 %fusion.2 = f32[8,2,64,256]{3,2,0,1:T(8,128)S(1)} fusion(s32[8,256]{1,0:T(8,128)S(1)} %copy-done.16, f32[16,1,2,64,256]{4,3,2,1,0:T(8,128)S(1)} %get-tuple-element.42, s32[]{:T(128)S(6)} %select_n.30), kind=kOutput, calls=%fused_computation.5 | convolution fusion | flops 805830656 | bytes 2105348 | tf_op jit(solution)/shard_map/bpik,bjk->bpij/dot_general | solution.py:33
  87.5 0.1 slice_bitcast_fusion
  87.6 0.6 convolution_subtract_fusion
  88.2 0.6 convolution_subtract_fusion.1
  88.8 1.6 %fusion = f32[8,2,64,256]{3,2,1,0:T(8,128)S(1)} fusion(f32[16,1,2,64,256]{4,3,2,1,0:T(8,128)S(1)} %get-tuple-element.43, s32[]{:T(128)S(6)} %select_n.28, s32[8,256]{1,0:T(8,128)S(1)} %copy-done.16), kind=kOutput, calls=%fused_computation.3 | convolution fusion | flops 805830656 | bytes 2105348 | tf_op jit(solution)/shard_map/bpik,bjk->bpij/dot_general | solution.py:33
  90.4 0.1 slice_bitcast_fusion.2
  90.5 0.6 convolution_subtract_fusion.2
  91.1 0.6 convolution_subtract_fusion.3
  91.7 0.7 convolution_subtract_fusion.10
  92.4 1.4 %convolution_subtract_fusion.12 = f32[8,64,64]{1,2,0:T(8,128)} fusion(f32[8,64,192]{2,1,0:T(8,128)S(1)} %all_gather.14, f32[8,64,192]{2,1,0:T(8,128)S(1)} %convolution_subtract_fusion.2, f32[8,64,256]{2,1,0:T(8,128)S(1)} %get-tuple-element.48), kind=kOutput, calls=%fused_computation.21 | convolution fusion | flops 75530240 | bytes 1048576 | tf_op jit(solution)/shard_map/bij,bkj->bik/dot_general | solution.py:33
  93.8 1.4 %convolution_subtract_fusion.9 = f32[8,64,64]{1,2,0:T(8,128)} fusion(f32[8,192,64]{1,2,0:T(8,128)S(1)} %all_gather.15, f32[8,64,192]{2,1,0:T(8,128)S(1)} %convolution_subtract_fusion.1, f32[8,64,256]{2,1,0:T(8,128)S(1)} %get-tuple-element.47), kind=kOutput, calls=%fused_computation.18 | convolution fusion | flops 75530240 | bytes 1048576 | tf_op jit(solution)/shard_map/bji,bkj->bik/dot_general | solution.py:33
  95.1 2.7 %fusion.54 = f32[8,64,192]{2,1,0:T(8,128)S(1)} fusion(f32[8,64,192]{2,1,0:T(8,128)S(1)} %convolution_subtract_fusion.3, f32[8,192,192]{2,1,0:T(8,128)} %all-gather.2.cloned.1.call-done), kind=kOutput, calls=%fused_computation.90 | convolution fusion | flops 226492416 | bytes 1966080 | tf_op jit(solution)/shard_map/bij,bjk->bik/dot_general | solution.py:33
  97.9 0.6 convolution_dynamic-update-slice_fusion
  98.6 1.1 fusion.55
  99.7 0.6 fusion.4
  100.4 2.2 %collective-permute-start.2 = (f32[4,64,64]{2,1,0:T(8,128)S(1)}, f32[4,64,64]{2,1,0:T(8,128)S(1)}, u32[]{:S(2)}, u32[]{:S(2)}) collective-permute-start(f32[4,64,64]{2,1,0:T(8,128)S(1)} %get-tuple-element.51), channel_id=1, source_target_pairs={{4,0},{8,4},{12,8},{16,12},{20,16},{24,20},{28,24},{0,28},{5,1},{9... | collective-permute-start | bytes 196616 | tf_op jit(solution)/shard_map/ppermute | solution.py:29
  102.6 0.7 convolution_subtract_fusion.11
  103.4 2.8 %collective-permute-done.2 = f32[4,64,64]{2,1,0:T(8,128)S(1)} collective-permute-done((f32[4,64,64]{2,1,0:T(8,128)S(1)}, f32[4,64,64]{2,1,0:T(8,128)S(1)}, u32[]{:S(2)}, u32[]{:S(2)}) %collective-permute-start.2) | collective-permute-done | bytes 65568 | tf_op jit(solution)/shard_map/ppermute | solution.py:29
  106.2 5.3 %collective-permute-done.3 = f32[4,64,64]{2,1,0:T(8,128)S(1)} collective-permute-done((f32[4,64,64]{2,1,0:T(8,128)S(1)}, f32[4,64,64]{2,1,0:T(8,128)S(1)}, u32[]{:S(2)}, u32[]{:S(2)}) %collective-permute-start.3) | collective-permute-done | bytes 65568 | tf_op jit(solution)/shard_map/ppermute | solution.py:29
  111.6 0.1 collective-permute-start.4
  111.7 0.1 maximum_bitcast_fusion
  111.8 1.4 %collective-permute-done.4 = f32[8,64,64]{2,1,0:T(8,128)S(1)} collective-permute-done((f32[8,64,64]{2,1,0:T(8,128)S(1)}, f32[8,64,64]{2,1,0:T(8,128)S(1)}, u32[]{:S(2)}, u32[]{:S(2)}) %collective-permute-start.4) | collective-permute-done | bytes 131104 | tf_op jit(solution)/shard_map/ppermute | solution.py:133
  113.2 1.4 %collective-permute-start.5 = (f32[8,64,64]{2,1,0:T(8,128)S(1)}, f32[8,64,64]{2,1,0:T(8,128)S(1)}, u32[]{:S(2)}, u32[]{:S(2)}) collective-permute-start(f32[8,64,64]{2,1,0:T(8,128)S(1)} %add.75), channel_id=1, source_target_pairs={{0,2},{1,3},{2,0},{3,1},{4,6},{5,7},{6,4},{7,5},{8,10},{9,11},{10,... | collective-permute-start | bytes 393224 | tf_op jit(solution)/shard_map/ppermute | solution.py:133
  114.6 1.1 pad_maximum_fusion.1
  115.6 2.3 %copy.87 = f32[8,2,64,128]{3,2,1,0:T(8,128)} copy(f32[8,2,64,128]{2,3,0,1:T(8,128)} %pad_maximum_fusion.1) | data formatting | bytes 1048576
  118.0 0.8 constant_dynamic-slice_fusion
  118.8 2.8 %collective-permute-done.5 = f32[8,64,64]{2,1,0:T(8,128)S(1)} collective-permute-done((f32[8,64,64]{2,1,0:T(8,128)S(1)}, f32[8,64,64]{2,1,0:T(8,128)S(1)}, u32[]{:S(2)}, u32[]{:S(2)}) %collective-permute-start.5) | collective-permute-done | bytes 131104 | tf_op jit(solution)/shard_map/ppermute | solution.py:133
  121.6 0.7 add_subtract_fusion
  (49 shorter events, 0.4 us)
Async XLA Ops:
  7.2 18.5 %copy-start = (f32[8,64,192]{2,1,0:T(8,128)S(1)}, f32[8,64,192]{2,1,0:T(8,128)}, u32[]{:S(2)}) copy-start(f32[8,64,192]{2,1,0:T(8,128)} %param.11) | copy-start | bytes 1179652
  7.2 15.8 %all-to-all-start = ((f32[8,64,256]{2,1,0:T(8,128)}), f32[8,64,256]{2,1,0:T(8,128)S(1)}, u32[]{:S(2)}, u32[]{:S(2)}) async-start(f32[8,64,256]{2,1,0:T(8,128)} %param.9), calls=%async_computation | async-start | bytes 1048576 | tf_op jit(solution)/shard_map/all_to_all | solution.py:97
  11.6 83.6 %all-gather.2.cloned.1.call-start = ((), (), s32[]{:S(2)}) async-start(), calls=%async_computation.1 | async-start | bytes 1966080 | tf_op jit(solution)/shard_map/all_gather | solution.py:102
  14.2 7.6 %copy-start.16 = (s32[8,256]{1,0:T(8,128)S(1)}, s32[8,256]{1,0:T(8,128)}, u32[]{:S(2)}) copy-start(s32[8,256]{1,0:T(8,128)} %param.10) | copy-start | bytes 24580
  15.8 67.7 %collective-permute-start = (f32[4,2,2,64,256]{4,3,2,1,0:T(8,128)}, f32[4,2,2,64,256]{4,3,2,1,0:T(8,128)}, u32[]{:S(2)}, u32[]{:S(2)}) collective-permute-start(f32[4,2,2,64,256]{4,3,2,1,0:T(8,128)} %get-tuple-element.44), channel_id=1, source_target_pairs={{0,4},{4,8},{8,12},{12,16},{16,20},{20,24},{24,28},{28,0},{1,5},{5... | collective-permute-start | bytes 3145736 | tf_op jit(solution)/shard_map/ppermute | solution.py:18
  18.1 65.4 %collective-permute-start.1 = (f32[4,2,2,64,256]{4,3,2,1,0:T(8,128)}, f32[4,2,2,64,256]{4,3,2,1,0:T(8,128)}, u32[]{:S(2)}, u32[]{:S(2)}) collective-permute-start(f32[4,2,2,64,256]{4,3,2,1,0:T(8,128)} %get-tuple-element.45), channel_id=1, source_target_pairs={{4,0},{8,4},{12,8},{16,12},{20,16},{24,20},{28,24},{0,28},{5,1},{9... | collective-permute-start | bytes 3145736 | tf_op jit(solution)/shard_map/ppermute | solution.py:21
  46.0 3.0 %copy-start.15 = (f32[192,192]{1,0:T(8,128)S(1)}, f32[192,192]{1,0:T(8,128)}, u32[]{:S(2)}) copy-start(f32[192,192]{1,0:T(8,128)} %fusion.25) | copy-start | bytes 442372
  51.8 2.1 %copy-start.2 = (f32[2,192,192]{2,1,0:T(8,128)}, f32[2,192,192]{2,1,0:T(8,128)S(1)}, u32[]{:S(2)}) copy-start(f32[2,192,192]{2,1,0:T(8,128)S(1)} %convolution_subtract_fusion.6) | copy-start | bytes 884740
  53.9 21.6 %copy-start.3 = (f32[2,192,192]{2,1,0:T(8,128)S(1)}, f32[2,192,192]{2,1,0:T(8,128)}, u32[]{:S(2)}) copy-start(f32[2,192,192]{2,1,0:T(8,128)} %copy-done.2) | copy-start | bytes 884740
  88.2 3.5 %copy-start.8 = (f32[8,64,192]{2,1,0:T(8,128)}, f32[8,64,192]{2,1,0:T(8,128)S(1)}, u32[]{:S(2)}) copy-start(f32[8,64,192]{2,1,0:T(8,128)S(1)} %convolution_subtract_fusion) | copy-start | bytes 1179652
  88.8 4.9 %copy-start.4 = (f32[8,64,192]{2,1,0:T(8,128)}, f32[8,64,192]{2,1,0:T(8,128)S(1)}, u32[]{:S(2)}) copy-start(f32[8,64,192]{2,1,0:T(8,128)S(1)} %convolution_subtract_fusion.1) | copy-start | bytes 1179652
  90.5 1.9 %copy-start.10 = (f32[8,64,256]{2,1,0:T(8,128)}, f32[8,64,256]{2,1,0:T(8,128)S(1)}, u32[]{:S(2)}) copy-start(f32[8,64,256]{2,1,0:T(8,128)S(1)} %get-tuple-element.49) | copy-start | bytes 1572868
  91.1 2.6 %copy-start.6 = (f32[8,64,192]{2,1,0:T(8,128)}, f32[8,64,192]{2,1,0:T(8,128)S(1)}, u32[]{:S(2)}) copy-start(f32[8,64,192]{2,1,0:T(8,128)S(1)} %convolution_subtract_fusion.2) | copy-start | bytes 1179652
  95.1 2.7 %copy-start.7 = (f32[8,64,192]{2,1,0:T(8,128)S(1)}, f32[8,64,192]{2,1,0:T(8,128)}, u32[]{:S(2)}) copy-start(f32[8,64,192]{2,1,0:T(8,128)} %copy-done.6) | copy-start | bytes 1179652
  95.1 3.4 %copy-start.1 = (f32[8,192,192]{2,1,0:T(8,128)S(1)}, f32[8,192,192]{2,1,0:T(8,128)}, u32[]{:S(2)}) copy-start(f32[8,192,192]{2,1,0:T(8,128)} %all-gather.2.cloned.1.call-done) | copy-start | bytes 3538948
  95.1 3.4 %copy-start.5 = (f32[8,64,192]{2,1,0:T(8,128)S(1)}, f32[8,64,192]{2,1,0:T(8,128)}, u32[]{:S(2)}) copy-start(f32[8,64,192]{2,1,0:T(8,128)} %copy-done.4) | copy-start | bytes 1179652
  97.9 1.8 %copy-start.9 = (f32[8,64,192]{2,1,0:T(8,128)S(1)}, f32[8,64,192]{2,1,0:T(8,128)}, u32[]{:S(2)}) copy-start(f32[8,64,192]{2,1,0:T(8,128)} %copy-done.8) | copy-start | bytes 1179652
  98.5 4.1 %copy-start.11 = (f32[8,64,256]{2,1,0:T(8,128)S(1)}, f32[8,64,256]{2,1,0:T(8,128)}, u32[]{:S(2)}) copy-start(f32[8,64,256]{2,1,0:T(8,128)} %copy-done.10) | copy-start | bytes 1572868
  100.3 11.3 %copy-start.13 = (f32[8,64,64]{1,2,0:T(8,128)S(1)}, f32[8,64,64]{1,2,0:T(8,128)}, u32[]{:S(2)}) copy-start(f32[8,64,64]{1,2,0:T(8,128)} %convolution_subtract_fusion.12) | copy-start | bytes 393220
  100.4 11.3 %copy-start.14 = (f32[8,64,64]{1,2,0:T(8,128)S(1)}, f32[8,64,64]{1,2,0:T(8,128)}, u32[]{:S(2)}) copy-start(f32[8,64,64]{1,2,0:T(8,128)} %convolution_subtract_fusion.9) | copy-start | bytes 393220
  100.4 5.8 %collective-permute-start.2 = (f32[4,64,64]{2,1,0:T(8,128)S(1)}, f32[4,64,64]{2,1,0:T(8,128)S(1)}, u32[]{:S(2)}, u32[]{:S(2)}) collective-permute-start(f32[4,64,64]{2,1,0:T(8,128)S(1)} %get-tuple-element.51), channel_id=1, source_target_pairs={{4,0},{8,4},{12,8},{16,12},{20,16},{24,20},{28,24},{0,28},{5,1},{9... | collective-permute-start | bytes 196616 | tf_op jit(solution)/shard_map/ppermute | solution.py:29
  103.3 8.2 %collective-permute-start.3 = (f32[4,64,64]{2,1,0:T(8,128)S(1)}, f32[4,64,64]{2,1,0:T(8,128)S(1)}, u32[]{:S(2)}, u32[]{:S(2)}) collective-permute-start(f32[4,64,64]{2,1,0:T(8,128)S(1)} %get-tuple-element.50), channel_id=1, source_target_pairs={{28,0},{0,4},{4,8},{8,12},{12,16},{16,20},{20,24},{24,28},{29,1},{... | collective-permute-start | bytes 196616 | tf_op jit(solution)/shard_map/ppermute | solution.py:29
  111.6 1.6 %collective-permute-start.4 = (f32[8,64,64]{2,1,0:T(8,128)S(1)}, f32[8,64,64]{2,1,0:T(8,128)S(1)}, u32[]{:S(2)}, u32[]{:S(2)}) collective-permute-start(f32[8,64,64]{2,1,0:T(8,128)S(1)} %fusion.26), channel_id=1, source_target_pairs={{0,1},{1,0},{2,3},{3,2},{4,5},{5,4},{6,7},{7,6},{8,9},{9,8},{10,11... | collective-permute-start | bytes 393224 | tf_op jit(solution)/shard_map/ppermute | solution.py:133
  113.2 8.4 %collective-permute-start.5 = (f32[8,64,64]{2,1,0:T(8,128)S(1)}, f32[8,64,64]{2,1,0:T(8,128)S(1)}, u32[]{:S(2)}, u32[]{:S(2)}) collective-permute-start(f32[8,64,64]{2,1,0:T(8,128)S(1)} %add.75), channel_id=1, source_target_pairs={{0,2},{1,3},{2,0},{3,1},{4,6},{5,7},{6,4},{7,5},{8,10},{9,11},{10,... | collective-permute-start | bytes 393224 | tf_op jit(solution)/shard_map/ppermute | solution.py:133
  114.6 7.0 %copy-start.12 = (f32[8,64,64]{2,1,0:T(8,128)S(1)}, f32[8,64,64]{2,1,0:T(8,128)}, u32[]{:S(2)}) copy-start(f32[8,64,64]{2,1,0:T(8,128)} %all_gather.12) | copy-start | bytes 393220
Sparse Core Ops, SparseCore 0:
  54.0 20.9 all-gather.1
